TPU v7x, 256 devices: a whole 4x4x8 slice. The times are simulated.
256 devices in a mesh: seq: 32 (over z, x), dp: 8 (over y, core).
Axes of the slice: x: 4, y: 4, z: 8, core: 2. Of those that a mesh axis runs over, the one named last changes fastest.
Arguments:
- tokens: bfloat16 [8, 16384, 4096], P('dp', 'seq'), may hold values from -6 to 6
- w_in: bfloat16 [4096, 2336], P(('seq', 'dp')), may hold values from -0.09375 to 0.09375
- conv_w: float32 [4, 2304], replicated, may hold values from -3 to 3
- a_rate: float32 [32], replicated, may hold values from 3.0517579e-06 to 0.06
- d_skip: float32 [32], replicated, may hold values from 0.5 to 2
- level_w: int32 [8, 11], P('dp'), may hold values from 0 to 256
- lengths: int32 [8], P('dp'), may hold values from 64 to 16384, as said below
Outputs:
- mixed_out: bfloat16 [8, 16384, 2048], P('dp', 'seq')
Inputs may be any that keep to these rules, and one draw needn't show every extreme that they name: `lengths`: every length is a multiple of 64, and some request has all 16384 positions live.
All inputs are finite; a program needn't handle non-finite values.
Results may differ from a plain program's by a relative error of at most 0.015.
Values may be sent and summed in bfloat16 or wider, within the bound.
No kernel may reach another device: no remote copies, remote signals or barrier semaphores. Data moves between devices by JAX's collectives and lax.ppermute only.
A program may use at most 128 MiB of HBM per device.

v0:
```python
import jax
import jax.numpy as jnp
import numpy as np
from jax import lax
from jax.sharding import PartitionSpec as P

STATE = 128
Q = 64


def passed_along(array, axis, by):
    count = lax.axis_size(axis)
    pairs = [(i, i + by) for i in range(count) if 0 <= i + by < count]
    return lax.ppermute(array, axis, pairs)


def swapped(value, axis, stride):
    mask = 2**stride
    pairs = [(source, source ^ mask) for source in range(lax.axis_size(axis))]
    return lax.ppermute(value, axis, pairs)


def body(tokens, w_in, conv_w, a_rate, d_skip, level_w, lengths):
    token_rows = tokens.reshape(-1, tokens.shape[-1])
    count = token_rows.shape[0]
    projected = jnp.dot(
        token_rows,
        lax.all_gather(w_in, ("seq", "dp"), axis=0, tiled=True),
        preferred_element_type=jnp.float32,
    )
    kernel = conv_w.shape[0]
    channels = conv_w.shape[1]
    heads = a_rate.shape[0]
    inner = channels - 2 * STATE
    raw = projected[:, :channels].astype(jnp.bfloat16)
    rim = passed_along(raw[count - (kernel - 1) :], "seq", 1)
    padded = jnp.concatenate([rim, raw], 0)
    convolved = jnp.zeros((count, channels), jnp.float32)
    for offset in range(kernel):
        convolved = convolved + padded[offset : offset + count].astype(jnp.float32) * conv_w[offset]
    values = jax.nn.silu(convolved[:, :inner]).astype(jnp.bfloat16)
    in_b = convolved[:, inner : inner + STATE].astype(jnp.bfloat16)
    out_c = convolved[:, inner + STATE :].astype(jnp.bfloat16)
    step_size = jax.nn.softplus(projected[:, channels:])
    log_decay = -step_size * a_rate[None, :]
    head_dim = inner // heads
    driven = (
        values.astype(jnp.float32).reshape(count, heads, head_dim) * step_size[:, :, None]
    ).astype(jnp.bfloat16)
    stretches = count // Q
    cumul = jnp.cumsum(log_decay.reshape(stretches, Q, heads), axis=1)
    totals = cumul[:, -1]
    before = jnp.cumsum(totals, axis=0) - totals
    level_wt = level_w.reshape(-1).astype(jnp.float32) / 256.0
    keys_b = in_b.reshape(stretches, Q, STATE)
    query_c = out_c.reshape(stretches, Q, STATE)
    drive_c = driven.reshape(stretches, Q, heads, head_dim)
    scores = jnp.einsum("ctn,csn->cts", query_c, keys_b, preferred_element_type=jnp.float32)
    causal = jnp.asarray(np.tril(np.ones((Q, Q), bool)))[None, :, :, None]
    differ = cumul[:, :, None, :] - cumul[:, None, :, :]
    inner_wt = (
        jnp.where(causal, jnp.exp(jnp.where(causal, differ, 0.0)), 0.0)
        * scores[..., None]
        * level_wt[0]
    )
    inner_wt = inner_wt.astype(jnp.bfloat16)
    y_inner = jnp.einsum("ctsh,cshp->cthp", inner_wt, drive_c, preferred_element_type=jnp.float32)
    to_end = jnp.exp(totals[:, None, :] - cumul)
    weighted_b = (keys_b.astype(jnp.float32)[:, :, None, :] * to_end[..., None]).astype(
        jnp.bfloat16
    )
    states = jnp.einsum("cshn,cshp->chnp", weighted_b, drive_c, preferred_element_type=jnp.float32)
    local_bits = stretches.bit_length() - 1
    carried = jnp.zeros_like(states)
    block_states = states
    block_decay = totals
    stretch_ids = np.arange(stretches)
    for level in range(local_bits):
        span = 2**level
        repeated = jnp.repeat(block_states, span, axis=0)
        previous = jnp.concatenate(
            [jnp.zeros_like(repeated[:span]), repeated[: stretches - span]], 0
        )
        bit_set = jnp.asarray((stretch_ids >> level & 1).astype(np.float32))
        aligned = stretch_ids >> level << level
        factor = bit_set[:, None] * level_wt[level + 1] * jnp.exp(before - before[aligned])
        carried = carried + factor[:, :, None, None] * previous
        block_states = (
            block_states[0::2] * jnp.exp(block_decay[1::2])[:, :, None, None] + block_states[1::2]
        )
        block_decay = block_decay[0::2] + block_decay[1::2]
    block_state = block_states[0]
    block_total = block_decay[0]
    position = lax.axis_index("seq")
    cross_state = jnp.zeros_like(block_state)
    passed = jnp.zeros_like(block_total)
    seq_bits = lax.axis_size("seq").bit_length() - 1
    for level in range(seq_bits):
        other_state, other_total = (
            swapped(block_state.astype(jnp.bfloat16), "seq", level).astype(block_state.dtype),
            swapped(block_total.astype(jnp.bfloat16), "seq", level).astype(block_total.dtype),
        )
        upper = (jnp.right_shift(position, level) & 1).astype(jnp.float32)
        cross_state = (
            cross_state
            + upper
            * level_wt[local_bits + level + 1]
            * jnp.exp(passed)[:, None, None]
            * other_state
        )
        passed = passed + upper * other_total
        block_state = jnp.where(
            upper > 0.5,
            other_state * jnp.exp(block_total)[:, None, None] + block_state,
            block_state * jnp.exp(other_total)[:, None, None] + other_state,
        )
        block_total = block_total + other_total
    carried = carried + jnp.exp(before)[:, :, None, None] * cross_state[None]
    carried_low = carried.astype(jnp.bfloat16)
    y_cross = jnp.exp(cumul)[..., None] * jnp.einsum(
        "ctn,chnp->cthp", query_c, carried_low, preferred_element_type=jnp.float32
    )
    output = (
        y_inner
        + y_cross
        + d_skip[None, None, :, None]
        * values.astype(jnp.float32).reshape(stretches, Q, heads, head_dim)
    )
    output = output * lax.rsqrt(jnp.mean(output * output, axis=-1, keepdims=True) + 1e-05)
    places = (position * count + jnp.arange(count, dtype=jnp.int32)).reshape(stretches, Q)
    output = jnp.where((places < lengths[0])[:, :, None, None], output, 0.0)
    return output.reshape(1, count, inner).astype(jnp.bfloat16)


def solution(mesh):
    in_specs = (P("dp", "seq", None), P(("seq", "dp"), None), P(), P(), P(), P("dp", None), P("dp"))
    out_specs = P("dp", "seq", None)
    return jax.shard_map(body, mesh=mesh, in_specs=in_specs, out_specs=out_specs, check_vma=False)
```

profile of v0, /device:TPU:5, one launch (start us, length us, event | category | flops | bytes accessed | tf_op | source)
XLA Modules:
  0.0 375.2 jit_solution(5178389369494430748)
XLA Ops:
  9.6 133.8 %all-gather.2.cloned.1.call-done = bf16[4096,2336]{1,0:T(8,128)(2,1)} async-done(((bf16[16,2336]{1,0:T(8,128)(2,1)}), bf16[4096,2336]{1,0:T(8,128)(2,1)}) %all-gather.2.cloned.1.call-update) | async-done | bytes 19136528 | tf_op jit(solution)/shard_map/all_gather | solution.py:28
  143.4 18.0 %fusion.50 = (bf16[512,2336]{0,1:T(8,128)(2,1)S(1)}, f32[512,2336]{0,1:T(8,128)}) fusion(bf16[4096,2336]{1,0:T(8,128)(2,1)} %all-gather.2.cloned.1.call-done, bf16[1,512,4096]{2,1,0:T(8,128)(2,1)} %param.17), kind=kOutput, calls=%fused_computation.119 | convolution fusion | flops 9799090176 | bytes 30507008 | tf_op jit(solution)/shard_map/dot_general | solution.py:26
  162.6 6.3 %fusion.51 = f32[8,64,32]{2,0,1:T(8,128)S(1)} fusion(f32[8,64,32]{2,0,1:T(8,128)S(1)} %copy.43), kind=kOutput, calls=%fused_computation.120 | output fusion | flops 1032192 | bytes 131072 | tf_op jit(solution)/shard_map/jit(cumsum)/reduce_window_sum | solution.py:51
  170.4 3.1 collective-permute-start
  177.2 5.9 %fusion.44 = (bf16[512,2304]{0,1:T(8,128)(2,1)S(1)}, f32[512,2304]{0,1:T(8,128)}) fusion(f32[2304]{0:T(1024)S(1)} %get-tuple-element.7, bf16[512,2304]{0,1:T(8,128)(2,1)S(1)} %slice.189, f32[2304]{0:T(1024)S(1)} %get-tuple-element.8, bf16[3,2304]{0,1:T(8,128)(2,1)S(1)} %copy.40, f32[2304]{0:T(1024)S(1)} %get-tuple-element.6, f32[2304]{0:T(1024)S(1)} %get-tuple-element.5), kind=kLoop, calls=%fused_computation.113 | loop fusion | flops 24772608 | bytes 9487872 | tf_op jit(solution)/shard_map/convert.2
  183.9 5.3 %fusion.15 = f32[512,2048]{0,1:T(8,128)} fusion(f32[512,2304]{0,1:T(8,128)} %get-tuple-element.20), kind=kLoop, calls=%fused_computation.33 | loop fusion | flops 6291456 | bytes 8388608 | tf_op jit(solution)/shard_map/reshape | solution.py:48
  189.2 7.2 %reshape.221 = f32[8,64,32,64]{1,0,3,2:T(8,128)} reshape(f32[512,2048]{0,1:T(8,128)} %fusion.15) | data formatting | bytes 8388608 | tf_op jit(solution)/shard_map/reshape | solution.py:48
  196.4 6.3 %fusion.2 = f32[8,32,128,64]{2,3,1,0:T(8,128)S(1)} fusion(f32[8,64,32]{1,2,0:T(8,128)S(1)} %copy.49, f32[8,64,128]{2,1,0:T(8,128)S(1)} %convert_element_type.135, f32[8,64,32,64]{1,0,3,2:T(8,128)} %reshape.221, f32[8,64,32]{1,2,0:T(8,128)S(1)} %copy-done.11), kind=kOutput, calls=%fused_computation.13 | convolution fusion | flops 274726912 | bytes 12976128 | tf_op jit(solution)/shard_map/cshn,cshp->chnp/dot_general | solution.py:72
  203.2 2.8 copy-done
  210.3 10.8 %collective-permute-done.2 = bf16[32]{0:T(256)(128)(2,1)S(1)} collective-permute-done((bf16[32]{0:T(256)(128)(2,1)S(1)}, bf16[32]{0:T(256)(128)(2,1)S(1)}, u32[]{:S(2)}, u32[]{:S(2)}) %collective-permute-start.2) | collective-permute-done | bytes 96 | tf_op jit(solution)/shard_map/ppermute | solution.py:20
  222.4 2.8 collective-permute-done.4
  232.0 9.9 %collective-permute-done.3 = bf16[32,128,64]{1,2,0:T(8,128)(2,1)S(1)} collective-permute-done((bf16[32,128,64]{1,2,0:T(8,128)(2,1)}, bf16[32,128,64]{1,2,0:T(8,128)(2,1)S(1)}, u32[]{:S(2)}, u32[]{:S(2)}) %collective-permute-start.3) | collective-permute-done | bytes 524320 | tf_op jit(solution)/shard_map/ppermute | solution.py:20
  245.7 6.5 %collective-permute-done.6 = bf16[32]{0:T(256)(128)(2,1)S(1)} collective-permute-done((bf16[32]{0:T(256)(128)(2,1)S(1)}, bf16[32]{0:T(256)(128)(2,1)S(1)}, u32[]{:S(2)}, u32[]{:S(2)}) %collective-permute-start.6) | collective-permute-done | bytes 96 | tf_op jit(solution)/shard_map/ppermute | solution.py:20
  264.6 20.6 %collective-permute-done.7 = bf16[32,128,64]{1,2,0:T(8,128)(2,1)S(1)} collective-permute-done((bf16[32,128,64]{1,2,0:T(8,128)(2,1)}, bf16[32,128,64]{1,2,0:T(8,128)(2,1)S(1)}, u32[]{:S(2)}, u32[]{:S(2)}) %collective-permute-start.7) | collective-permute-done | bytes 524320 | tf_op jit(solution)/shard_map/ppermute | solution.py:20
  287.8 3.0 collective-permute-start.9
  296.1 21.0 %collective-permute-done.9 = bf16[32,128,64]{1,2,0:T(8,128)(2,1)} collective-permute-done((bf16[32,128,64]{1,2,0:T(8,128)(2,1)}, bf16[32,128,64]{1,2,0:T(8,128)(2,1)}, u32[]{:S(2)}, u32[]{:S(2)}) %collective-permute-start.9) | collective-permute-done | bytes 524320 | tf_op jit(solution)/shard_map/ppermute | solution.py:20
  317.1 3.2 fusion.19
  320.3 4.0 %broadcast_in_dim.37 = f32[3,2,32,128,64]{3,4,2,1,0:T(8,128)} broadcast(f32[3,32,128,64]{2,3,1,0:T(8,128)S(1)} %slice-done.3), dimensions={0,2,3,4} | broadcast | bytes 9437184 | tf_op jit(solution)/shard_map/broadcast_in_dim | solution.py:80
  327.5 7.6 %add_convert_fusion = bf16[8,32,128,64]{2,3,1,0:T(8,128)(2,1)} fusion(f32[4,32,128,64]{2,3,1,0:T(8,128)} %slice.172, f32[6,32,128,64]{2,3,1,0:T(8,128)} %bitcast.73, f32[7,32,128,64]{2,3,1,0:T(8,128)S(1)} %slice-done, f32[32,128,64]{1,2,0:T(8,128)S(1)} %copy-done.4, f32[8,32]{1,0:T(8,128)S(1)} %get-tuple-element.9, f32[8,32]{1,0:T(8,128)S(1)} %get-tuple-element.30, ...), kind=kLoop, calls=%fused_computation.7 | loop fusion | flops 16777216 | bytes 23072768 | tf_op jit(solution)/shard_map/convert_element_type | solution.py:119
  335.1 3.5 fusion.53
  338.7 8.8 %multiply_reduce_fusion = (f32[8,64,32]{1,2,0:T(8,128)S(1)}, f32[8,64,32,64]{1,3,2,0:T(8,128)}) fusion(f32[8,64,32,64]{1,0,3,2:T(8,128)S(1)} %bitcast.70, f32[32]{0:T(128)S(1)} %copy-done.22, f32[8,64,32,64]{1,3,2,0:T(8,128)S(1)} %bitcast.72, f32[8,64,32]{1,2,0:T(8,128)S(1)} %copy-done.16, f32[]{:T(128)} %bitcast.4, f32[8,64,64]{2,1,0:T(8,128)S(1)} %copy-done.14, ...), kind=kOutput, calls=%fused_computation.6 | convolution fusion | flops 148881408 | bytes 12980356 | tf_op jit(solution)/shard_map/ctsh,cshp->cthp/dot_general | solution.py:67
  347.5 7.0 %select_convert_fusion = bf16[8,64,32,64]{1,3,2,0:T(8,128)(2,1)} fusion(f32[8,64,32,64]{1,3,2,0:T(8,128)} %get-tuple-element.60, f32[8,64,32]{1,2,0:T(8,128)S(1)} %add_rsqrt_fusion, pred[8,64]{1,0:T(8,128)(4,1)S(1)} %copy-done.17), kind=kLoop, calls=%fused_computation.5 | loop fusion | flops 3145728 | bytes 6357504 | tf_op jit(solution)/shard_map/convert_element_type | solution.py:132
  354.5 7.1 %copy.51 = bf16[8,64,32,64]{3,2,1,0:T(8,128)(2,1)} copy(bf16[8,64,32,64]{1,3,2,0:T(8,128)(2,1)} %select_convert_fusion) | data formatting | bytes 4194304 | tf_op jit(solution)/shard_map/convert_element_type | solution.py:132
  361.6 6.7 %convert_element_type.162 = bf16[1,512,2048]{2,1,0:T(8,128)(2,1)} reshape(bf16[8,64,32,64]{3,2,1,0:T(8,128)(2,1)} %copy.51) | data formatting | bytes 4194304 | tf_op jit(solution)/shard_map/convert_element_type | solution.py:132
  (128 shorter events, 46.8 us)
Async XLA Ops:
  6.5 136.9 %all-gather.2.cloned.1.call-start = ((), (), s32[]{:S(2)}) async-start(), calls=%async_computation | async-start | bytes 20000768 | tf_op jit(solution)/shard_map/all_gather | solution.py:28
  9.6 151.7 %copy-start.20 = (f32[32]{0:T(128)S(1)}, f32[32]{0:T(128)}, u32[]{:S(2)}) copy-start(f32[32]{0:T(128)} %param.20) | copy-start | bytes 388
  161.4 12.2 %copy-start.6 = (bf16[512,2336]{0,1:T(8,128)(2,1)}, bf16[512,2336]{0,1:T(8,128)(2,1)S(1)}, u32[]{:S(2)}) copy-start(bf16[512,2336]{0,1:T(8,128)(2,1)S(1)} %get-tuple-element.57) | copy-start | bytes 7176196
  169.9 36.3 %copy-start.19 = (f32[32]{0:T(128)}, f32[32]{0:T(128)S(1)}, u32[]{:S(2)}) copy-start(f32[32]{0:T(128)S(1)} %exponential_bitcast_fusion) | copy-start | bytes 388
  170.4 6.4 %collective-permute-start = (bf16[3,2304]{1,0:T(4,128)(2,1)S(1)}, bf16[3,2304]{1,0:T(4,128)(2,1)S(1)}, u32[]{:S(2)}, u32[]{:S(2)}) collective-permute-start(bf16[3,2304]{1,0:T(4,128)(2,1)S(1)} %copy.39), channel_id=1, source_target_pairs={{0,8},{8,16},{16,24},{24,32},{32,40},{40,48},{48,56},{56,64},{64,7... | collective-permute-start | bytes 41480 | tf_op jit(solution)/shard_map/ppermute | solution.py:14
  174.1 47.1 %copy-start.18 = (f32[1,32]{1,0:T(1,128)}, f32[1,32]{1,0:T(1,128)S(1)}, u32[]{:S(2)}) copy-start(f32[1,32]{1,0:T(1,128)S(1)} %get-tuple-element.18) | copy-start | bytes 388
  189.2 7.2 %copy-start.11 = (f32[8,64,32]{1,2,0:T(8,128)S(1)}, f32[8,64,32]{1,2,0:T(8,128)}, u32[]{:S(2)}) copy-start(f32[8,64,32]{1,2,0:T(8,128)} %copy.41) | copy-start | bytes 196612
  208.2 18.2 %collective-permute-start.1 = (bf16[32,128,64]{1,2,0:T(8,128)(2,1)S(1)}, bf16[32,128,64]{1,2,0:T(8,128)(2,1)S(1)}, u32[]{:S(2)}, u32[]{:S(2)}) collective-permute-start(bf16[32,128,64]{1,2,0:T(8,128)(2,1)S(1)} %get-tuple-element.25), channel_id=1, source_target_pairs={{0,8},{8,0},{16,24},{24,16},{32,40},{40,32},{48,56},{56,48},{64,72... | collective-permute-start | bytes 1572872 | tf_op jit(solution)/shard_map/ppermute | solution.py:20
  208.6 12.6 %collective-permute-start.2 = (bf16[32]{0:T(256)(128)(2,1)S(1)}, bf16[32]{0:T(256)(128)(2,1)S(1)}, u32[]{:S(2)}, u32[]{:S(2)}) collective-permute-start(bf16[32]{0:T(256)(128)(2,1)S(1)} %bitcast_convert_fusion), channel_id=1, source_target_pairs={{0,8},{8,0},{16,24},{24,16},{32,40},{40,32},{48,56},{56,48},{64,72... | collective-permute-start | bytes 200 | tf_op jit(solution)/shard_map/ppermute | solution.py:20
  221.2 4.0 %collective-permute-start.4 = (bf16[32]{0:T(256)(128)(2,1)S(1)}, bf16[32]{0:T(256)(128)(2,1)}, u32[]{:S(2)}, u32[]{:S(2)}) collective-permute-start(bf16[32]{0:T(256)(128)(2,1)S(1)} %fusion.36), channel_id=1, source_target_pairs={{0,16},{8,24},{16,0},{24,8},{32,48},{40,56},{48,32},{56,40},{64,80... | collective-permute-start | bytes 200 | tf_op jit(solution)/shard_map/ppermute | solution.py:20
  229.5 63.7 %copy-start.9 = (f32[8,64,32]{2,0,1:T(8,128)S(1)}, f32[8,64,32]{2,0,1:T(8,128)}, u32[]{:S(2)}) copy-start(f32[8,64,32]{2,0,1:T(8,128)} %get-tuple-element.27) | copy-start | bytes 196612
  229.5 12.4 %collective-permute-start.3 = (bf16[32,128,64]{1,2,0:T(8,128)(2,1)}, bf16[32,128,64]{1,2,0:T(8,128)(2,1)S(1)}, u32[]{:S(2)}, u32[]{:S(2)}) collective-permute-start(bf16[32,128,64]{1,2,0:T(8,128)(2,1)} %get-tuple-element.15), channel_id=1, source_target_pairs={{0,16},{8,24},{16,0},{24,8},{32,48},{40,56},{48,32},{56,40},{64,80... | collective-permute-start | bytes 1572872 | tf_op jit(solution)/shard_map/ppermute | solution.py:20
  241.9 52.2 %copy-start.2 = (bf16[32,128,64]{1,2,0:T(8,128)(2,1)}, bf16[32,128,64]{1,2,0:T(8,128)(2,1)S(1)}, u32[]{:S(2)}) copy-start(bf16[32,128,64]{1,2,0:T(8,128)(2,1)S(1)} %collective-permute-done.3) | copy-start | bytes 1572868
  242.3 15.1 %collective-permute-start.5 = (bf16[32,128,64]{1,2,0:T(8,128)(2,1)S(1)}, bf16[32,128,64]{1,2,0:T(8,128)(2,1)S(1)}, u32[]{:S(2)}, u32[]{:S(2)}) collective-permute-start(bf16[32,128,64]{1,2,0:T(8,128)(2,1)S(1)} %fusion.38), channel_id=1, source_target_pairs={{0,32},{8,40},{16,48},{24,56},{32,0},{40,8},{48,16},{56,24},{64,96... | collective-permute-start | bytes 1572872 | tf_op jit(solution)/shard_map/ppermute | solution.py:20
  244.0 8.2 %collective-permute-start.6 = (bf16[32]{0:T(256)(128)(2,1)S(1)}, bf16[32]{0:T(256)(128)(2,1)S(1)}, u32[]{:S(2)}, u32[]{:S(2)}) collective-permute-start(bf16[32]{0:T(256)(128)(2,1)S(1)} %convert_element_type.151), channel_id=1, source_target_pairs={{0,32},{8,40},{16,48},{24,56},{32,0},{40,8},{48,16},{56,24},{64,96... | collective-permute-start | bytes 200 | tf_op jit(solution)/shard_map/ppermute | solution.py:20
  252.8 3.3 collective-permute-start.8
  257.3 36.8 %copy-start.3 = (bf16[32,128,64]{1,2,0:T(8,128)(2,1)}, bf16[32,128,64]{1,2,0:T(8,128)(2,1)S(1)}, u32[]{:S(2)}) copy-start(bf16[32,128,64]{1,2,0:T(8,128)(2,1)S(1)} %collective-permute-done.5) | copy-start | bytes 1572868
  259.4 25.7 %collective-permute-start.7 = (bf16[32,128,64]{1,2,0:T(8,128)(2,1)}, bf16[32,128,64]{1,2,0:T(8,128)(2,1)S(1)}, u32[]{:S(2)}, u32[]{:S(2)}) collective-permute-start(bf16[32,128,64]{1,2,0:T(8,128)(2,1)} %fusion.37), channel_id=1, source_target_pairs={{0,64},{8,72},{16,80},{24,88},{32,96},{40,104},{48,112},{56,120},{... | collective-permute-start | bytes 1572872 | tf_op jit(solution)/shard_map/ppermute | solution.py:20
  287.8 29.3 %collective-permute-start.9 = (bf16[32,128,64]{1,2,0:T(8,128)(2,1)}, bf16[32,128,64]{1,2,0:T(8,128)(2,1)}, u32[]{:S(2)}, u32[]{:S(2)}) collective-permute-start(bf16[32,128,64]{1,2,0:T(8,128)(2,1)} %fusion.28), channel_id=1, source_target_pairs={{0,128},{8,136},{16,144},{24,152},{32,160},{40,168},{48,176},{56,1... | collective-permute-start | bytes 1572872 | tf_op jit(solution)/shard_map/ppermute | solution.py:20
  294.1 26.1 %slice-start.3 = ((f32[4,32,128,64]{2,3,1,0:T(8,128)}), f32[3,32,128,64]{2,3,1,0:T(8,128)S(1)}, s32[]{:S(2)}) async-start(f32[4,32,128,64]{2,3,1,0:T(8,128)} %copy-done.1), calls=%async_computation.4 | async-start | bytes 6291456 | tf_op jit(solution)/shard_map/slice | solution.py:82
  320.3 6.7 %slice-start = ((f32[8,32,128,64]{2,3,1,0:T(8,128)}), f32[7,32,128,64]{2,3,1,0:T(8,128)S(1)}, s32[]{:S(2)}) async-start(f32[8,32,128,64]{2,3,1,0:T(8,128)} %copy-done), calls=%async_computation.1 | async-start | bytes 14680064 | tf_op jit(solution)/shard_map/slice | solution.py:82
  324.3 14.3 %slice-start.1 = ((s8[8388608]{0:T(1024)(128)(4,1)}), s8[4194304]{0:T(1024)(128)(4,1)S(1)}, s32[]{:S(2)}) async-start(s8[8388608]{0:T(1024)(128)(4,1)} %bitcast.69), calls=%async_computation.2 | async-start | bytes 8388608
  327.5 11.2 %slice-start.2 = ((s8[8388608]{0:T(1024)(128)(4,1)}), s8[4194304]{0:T(1024)(128)(4,1)S(1)}, s32[]{:S(2)}) async-start(s8[8388608]{0:T(1024)(128)(4,1)} %bitcast.69), calls=%async_computation.3 | async-start | bytes 8388608
  338.7 8.8 %copy-start.17 = (pred[8,64]{1,0:T(8,128)(4,1)S(1)}, pred[8,64]{1,0:T(8,128)(4,1)}, u32[]{:S(2)}) copy-start(pred[8,64]{1,0:T(8,128)(4,1)} %add_compare_fusion) | copy-start | bytes 1540
  (15 other events, 45.9 us)
Sparse Core Ops, SparseCore 0:
  10.9 132.4 all-gather.1
where the time goes:
time: 376 us; the launch traced here: 375 us
  waiting for transfers between devices  208 us (55%)
  other arithmetic  56.9 us (15%)
  local copies, waits for them, and re-layouts  43.1 us (11%)
  matrix products  37.4 us (10%)
  between operations  17.3 us (5%)
  starting transfers between devices  12.8 us (3%)
    all_gather x1, waiting for transfers between devices, body(): lax.all_gather(w_in, ('seq', 'dp'), axis=0, tiled=True)  134 us
    ppermute x9, waiting for transfers between devices, swapped(): return lax.ppermute(value, axis, pairs)  73.2 us
    dot_general x1, matrix products, body(): jnp.dot(token_rows, lax.all_gather(w_in, ('seq', 'dp'), axis=0, tiled=Tru...  18 us
    convert_element_type x2, local copies, waits for them, and re-layouts, body(): return output.reshape(1, count, inner).astype(jnp.bfloat16)  13.9 us
    ppermute x9, starting transfers between devices, swapped(): return lax.ppermute(value, axis, pairs)  9.71 us
    dot_general x1, matrix products, body(): jnp.einsum('ctsh,cshp->cthp', inner_wt, drive_c, preferred_element_type=j...  8.75 us
    convert_element_type x5, other arithmetic, body(): block_state.astype(jnp.bfloat16)  8.74 us
    convert_element_type x1, other arithmetic, body(): carried_low = carried.astype(jnp.bfloat16)  7.62 us
  transfers between devices with their start and end apart: 11, of which 8 were waited for; matrix products, arithmetic and copies ran while one was open for 5% of the time, Pallas kernels for 0%

commit v1 on v0

--- a/solution.py
+++ b/solution.py
@@ -25,7 +25,10 @@
     count = token_rows.shape[0]
     projected = jnp.dot(
         token_rows,
-        lax.all_gather(w_in, ("seq", "dp"), axis=0, tiled=True),
+        jnp.concatenate(
+            lax.all_to_all(jnp.stack([w_in] * lax.axis_size(("seq", "dp"))), ("seq", "dp"), 0, 0),
+            axis=0,
+        ),
         preferred_element_type=jnp.float32,
     )
     kernel = conv_w.shape[0]

time: 376 us -> 680 us (1.81)
  waiting for transfers between devices: 208 us -> 493 us
  starting transfers between devices: 12.8 us -> 36.4 us
  between operations: 17.3 us -> 4.23 us
  local copies, waits for them, and re-layouts: 43.1 us -> 51.1 us
    all_to_all x0 -> x1, waiting for transfers between devices: none -> 429 us  [body(): lax.all_to_all(jnp.stack([w_in] * lax.axis_size(('seq', 'dp'))), ('seq',...]
    all_gather x1 -> x0, waiting for transfers between devices: 134 us -> none  [body(): lax.all_gather(w_in, ('seq', 'dp'), axis=0, tiled=True)]
    all_to_all x0 -> x1, starting transfers between devices: none -> 15.8 us  [body(): lax.all_to_all(jnp.stack([w_in] * lax.axis_size(('seq', 'dp'))), ('seq',...]
    ppermute x9, waiting for transfers between devices: 73.2 us -> 64.6 us  [swapped(): return lax.ppermute(value, axis, pairs)]
    ppermute x9, starting transfers between devices: 9.71 us -> 17.6 us  [swapped(): return lax.ppermute(value, axis, pairs)]
    another operation x1 -> x2, local copies, waits for them, and re-layouts: 0.01 us -> 7.64 us  [the longest x1 7.64 us: body(): jnp.stack([w_in] * lax.axis_size(('seq', 'dp')))]
  transfers between devices with their start and end apart: 11 -> 11, of which waited for: 8 -> 8; matrix products, arithmetic and copies ran while one was open for 5% -> 3% of each run, Pallas kernels for 0% -> 0%
where the time goes in v1:
time: 680 us; the launch traced here: 677 us
  waiting for transfers between devices  493 us (72%)
  other arithmetic  54.7 us (8%)
  local copies, waits for them, and re-layouts  51.1 us (8%)
  matrix products  37.2 us (5%)
  starting transfers between devices  36.4 us (5%)
    all_to_all x1, waiting for transfers between devices, body(): lax.all_to_all(jnp.stack([w_in] * lax.axis_size(('seq', 'dp'))), ('seq',...  429 us
    ppermute x9, waiting for transfers between devices, swapped(): return lax.ppermute(value, axis, pairs)  64.6 us
    dot_general x1, matrix products, body(): jnp.dot(token_rows, jnp.concatenate(lax.all_to_all(jnp.stack([w_in] * lax...  17.8 us
    ppermute x9, starting transfers between devices, swapped(): return lax.ppermute(value, axis, pairs)  17.6 us
    all_to_all x1, starting transfers between devices, body(): lax.all_to_all(jnp.stack([w_in] * lax.axis_size(('seq', 'dp'))), ('seq',...  15.8 us
    convert_element_type x2, local copies, waits for them, and re-layouts, body(): return output.reshape(1, count, inner).astype(jnp.bfloat16)  13.9 us
  transfers between devices with their start and end apart: 11, of which 8 were waited for; matrix products, arithmetic and copies ran while one was open for 3% of the time, Pallas kernels for 0%

profile of v1, /device:TPU:5, one launch (start us, length us, event | category | flops | bytes accessed | tf_op | source)
XLA Modules:
  0.0 677.0 jit_solution(8666359385752030047)
XLA Ops:
  0.0 7.6 %stack.2 = bf16[256,16,2336]{2,1,0:T(8,128)(2,1)} broadcast(bf16[16,2336]{1,0:T(8,128)(2,1)} %param.18), dimensions={1,2} | broadcast | bytes 19211264 | tf_op jit(solution)/shard_map/stack | solution.py:29
  7.6 15.8 %all-to-all-start = ((bf16[256,16,2336]{2,1,0:T(8,128)(2,1)}), bf16[256,16,2336]{2,1,0:T(8,128)(2,1)}, u32[]{:S(2)}, u32[]{:S(2)}) async-start(bf16[256,16,2336]{2,1,0:T(8,128)(2,1)} %stack.2), calls=%async_computation | async-start | bytes 39845888 | tf_op jit(solution)/shard_map/all_to_all | solution.py:29
  25.0 428.8 %all-to-all-done = bf16[256,16,2336]{2,1,0:T(8,128)(2,1)} async-done(((bf16[256,16,2336]{2,1,0:T(8,128)(2,1)}), bf16[256,16,2336]{2,1,0:T(8,128)(2,1)}, u32[]{:S(2)}, u32[]{:S(2)}) %all-to-all-start) | async-done | bytes 19136544 | tf_op jit(solution)/shard_map/all_to_all | solution.py:29
  453.7 17.8 %fusion.50 = (bf16[512,2336]{0,1:T(8,128)(2,1)S(1)}, f32[512,2336]{0,1:T(8,128)}) fusion(bf16[4096,2336]{1,0:T(8,128)(2,1)} %bitcast.2, bf16[1,512,4096]{2,1,0:T(8,128)(2,1)} %param.17), kind=kOutput, calls=%fused_computation.119 | convolution fusion | flops 9799090176 | bytes 30507008 | tf_op jit(solution)/shard_map/dot_general | solution.py:26
  472.8 6.3 fusion.51
  481.2 2.9 collective-permute-start
  487.7 5.9 fusion.44
  494.4 5.3 fusion.15
  499.7 7.2 %reshape.227 = f32[8,64,32,64]{1,0,3,2:T(8,128)} reshape(f32[512,2048]{0,1:T(8,128)} %fusion.15) | data formatting | bytes 8388608 | tf_op jit(solution)/shard_map/reshape | solution.py:51
  506.9 6.3 fusion.2
  513.7 2.8 copy-done
  521.7 9.4 %collective-permute-done.2 = bf16[32]{0:T(256)(128)(2,1)S(1)} collective-permute-done((bf16[32]{0:T(256)(128)(2,1)S(1)}, bf16[32]{0:T(256)(128)(2,1)S(1)}, u32[]{:S(2)}, u32[]{:S(2)}) %collective-permute-start.2) | collective-permute-done | bytes 96 | tf_op jit(solution)/shard_map/ppermute | solution.py:20
  543.0 7.4 %collective-permute-done.3 = bf16[32,128,64]{1,2,0:T(8,128)(2,1)S(1)} collective-permute-done((bf16[32,128,64]{1,2,0:T(8,128)(2,1)}, bf16[32,128,64]{1,2,0:T(8,128)(2,1)S(1)}, u32[]{:S(2)}, u32[]{:S(2)}) %collective-permute-start.3) | collective-permute-done | bytes 524320 | tf_op jit(solution)/shard_map/ppermute | solution.py:20
  554.2 4.9 collective-permute-done.6
  559.7 6.2 collective-permute-start.8
  576.4 19.1 %collective-permute-done.7 = bf16[32,128,64]{1,2,0:T(8,128)(2,1)S(1)} collective-permute-done((bf16[32,128,64]{1,2,0:T(8,128)(2,1)}, bf16[32,128,64]{1,2,0:T(8,128)(2,1)S(1)}, u32[]{:S(2)}, u32[]{:S(2)}) %collective-permute-start.7) | collective-permute-done | bytes 524320 | tf_op jit(solution)/shard_map/ppermute | solution.py:20
  605.6 21.0 %collective-permute-done.9 = bf16[32,128,64]{1,2,0:T(8,128)(2,1)} collective-permute-done((bf16[32,128,64]{1,2,0:T(8,128)(2,1)}, bf16[32,128,64]{1,2,0:T(8,128)(2,1)}, u32[]{:S(2)}, u32[]{:S(2)}) %collective-permute-start.9) | collective-permute-done | bytes 524320 | tf_op jit(solution)/shard_map/ppermute | solution.py:20
  631.1 4.2 broadcast_in_dim.37
  636.5 7.3 %add_convert_fusion = bf16[8,32,128,64]{2,3,1,0:T(8,128)(2,1)} fusion(f32[4,32,128,64]{2,3,1,0:T(8,128)} %slice.172, f32[6,32,128,64]{2,3,1,0:T(8,128)} %bitcast.74, f32[7,32,128,64]{2,3,1,0:T(8,128)S(1)} %slice-done, f32[32,128,64]{1,2,0:T(8,128)S(1)} %fusion.19, f32[8,32]{1,0:T(8,128)S(1)} %get-tuple-element.9, f32[8,32]{1,0:T(8,128)S(1)} %get-tuple-element.30, ...), kind=kLoop, calls=%fused_computation.7 | loop fusion | flops 16777216 | bytes 23072768 | tf_op jit(solution)/shard_map/convert_element_type | solution.py:122
  643.8 3.5 fusion.53
  647.4 8.7 %multiply_reduce_fusion = (f32[8,64,32]{1,2,0:T(8,128)S(1)}, f32[8,64,32,64]{1,3,2,0:T(8,128)}) fusion(f32[8,64,32,64]{1,0,3,2:T(8,128)S(1)} %bitcast.71, f32[32]{0:T(128)S(1)} %copy-done.21, f32[8,64,32,64]{1,3,2,0:T(8,128)S(1)} %bitcast.73, f32[8,64,32]{1,2,0:T(8,128)S(1)} %copy-done.13, f32[]{:T(128)} %bitcast.5, f32[8,64,64]{2,1,0:T(8,128)S(1)} %copy-done.11, ...), kind=kOutput, calls=%fused_computation.6 | convolution fusion | flops 148881408 | bytes 12980356 | tf_op jit(solution)/shard_map/ctsh,cshp->cthp/dot_general | solution.py:70
  656.1 7.0 %select_convert_fusion = bf16[8,64,32,64]{1,3,2,0:T(8,128)(2,1)} fusion(f32[8,64,32,64]{1,3,2,0:T(8,128)} %get-tuple-element.60, f32[8,64,32]{1,2,0:T(8,128)S(1)} %add_rsqrt_fusion, pred[8,64]{1,0:T(8,128)(4,1)S(1)} %copy-done.15), kind=kLoop, calls=%fused_computation.5 | loop fusion | flops 3145728 | bytes 6357504 | tf_op jit(solution)/shard_map/convert_element_type | solution.py:135
  663.1 7.1 %copy.51 = bf16[8,64,32,64]{3,2,1,0:T(8,128)(2,1)} copy(bf16[8,64,32,64]{1,3,2,0:T(8,128)(2,1)} %select_convert_fusion) | data formatting | bytes 4194304 | tf_op jit(solution)/shard_map/convert_element_type | solution.py:135
  670.2 6.7 convert_element_type.162
  (126 shorter events, 53.5 us)
Async XLA Ops:
  7.6 15.8 %copy-start.20 = (s32[1,11]{1,0:T(1,128)S(1)}, s32[1,11]{1,0:T(1,128)}, u32[]{:S(2)}) copy-start(s32[1,11]{1,0:T(1,128)} %param.22) | copy-start | bytes 136
  7.6 17.2 %copy-start.14 = (f32[4,2304]{1,0:T(4,128)S(1)}, f32[4,2304]{1,0:T(4,128)}, u32[]{:S(2)}) copy-start(f32[4,2304]{1,0:T(4,128)} %param.19) | copy-start | bytes 110596
  7.6 446.1 %all-to-all-start = ((bf16[256,16,2336]{2,1,0:T(8,128)(2,1)}), bf16[256,16,2336]{2,1,0:T(8,128)(2,1)}, u32[]{:S(2)}, u32[]{:S(2)}) async-start(bf16[256,16,2336]{2,1,0:T(8,128)(2,1)} %stack.2), calls=%async_computation | async-start | bytes 39845888 | tf_op jit(solution)/shard_map/all_to_all | solution.py:29
  453.7 17.8 %copy-start.18 = (f32[32]{0:T(128)S(1)}, f32[32]{0:T(128)}, u32[]{:S(2)}) copy-start(f32[32]{0:T(128)} %param.20) | copy-start | bytes 388
  471.6 12.5 %copy-start.3 = (bf16[512,2336]{0,1:T(8,128)(2,1)}, bf16[512,2336]{0,1:T(8,128)(2,1)S(1)}, u32[]{:S(2)}) copy-start(bf16[512,2336]{0,1:T(8,128)(2,1)S(1)} %get-tuple-element.57) | copy-start | bytes 7176196
  480.7 50.4 %copy-start.16 = (f32[1,32]{1,0:T(1,128)}, f32[1,32]{1,0:T(1,128)S(1)}, u32[]{:S(2)}) copy-start(f32[1,32]{1,0:T(1,128)S(1)} %get-tuple-element.18) | copy-start | bytes 388
  481.2 6.2 collective-permute-start
  499.7 7.2 %copy-start.8 = (f32[8,64,32]{1,2,0:T(8,128)S(1)}, f32[8,64,32]{1,2,0:T(8,128)}, u32[]{:S(2)}) copy-start(f32[8,64,32]{1,2,0:T(8,128)} %copy.41) | copy-start | bytes 196612
  518.7 17.6 %collective-permute-start.1 = (bf16[32,128,64]{1,2,0:T(8,128)(2,1)S(1)}, bf16[32,128,64]{1,2,0:T(8,128)(2,1)S(1)}, u32[]{:S(2)}, u32[]{:S(2)}) collective-permute-start(bf16[32,128,64]{1,2,0:T(8,128)(2,1)S(1)} %get-tuple-element.25), channel_id=1, source_target_pairs={{0,8},{8,0},{16,24},{24,16},{32,40},{40,32},{48,56},{56,48},{64,72... | collective-permute-start | bytes 1572872 | tf_op jit(solution)/shard_map/ppermute | solution.py:20
  521.1 10.0 %collective-permute-start.2 = (bf16[32]{0:T(256)(128)(2,1)S(1)}, bf16[32]{0:T(256)(128)(2,1)S(1)}, u32[]{:S(2)}, u32[]{:S(2)}) collective-permute-start(bf16[32]{0:T(256)(128)(2,1)S(1)} %bitcast_convert_fusion), channel_id=1, source_target_pairs={{0,8},{8,0},{16,24},{24,16},{32,40},{40,32},{48,56},{56,48},{64,72... | collective-permute-start | bytes 200 | tf_op jit(solution)/shard_map/ppermute | solution.py:20
  531.1 4.0 collective-permute-start.4
  539.4 63.4 %copy-start.6 = (f32[8,64,32]{2,0,1:T(8,128)S(1)}, f32[8,64,32]{2,0,1:T(8,128)}, u32[]{:S(2)}) copy-start(f32[8,64,32]{2,0,1:T(8,128)} %get-tuple-element.27) | copy-start | bytes 196612
  539.4 10.9 %collective-permute-start.3 = (bf16[32,128,64]{1,2,0:T(8,128)(2,1)}, bf16[32,128,64]{1,2,0:T(8,128)(2,1)S(1)}, u32[]{:S(2)}, u32[]{:S(2)}) collective-permute-start(bf16[32,128,64]{1,2,0:T(8,128)(2,1)} %get-tuple-element.15), channel_id=1, source_target_pairs={{0,16},{8,24},{16,0},{24,8},{32,48},{40,56},{48,32},{56,40},{64,80... | collective-permute-start | bytes 1572872 | tf_op jit(solution)/shard_map/ppermute | solution.py:20
  550.7 17.5 %collective-permute-start.5 = (bf16[32,128,64]{1,2,0:T(8,128)(2,1)S(1)}, bf16[32,128,64]{1,2,0:T(8,128)(2,1)S(1)}, u32[]{:S(2)}, u32[]{:S(2)}) collective-permute-start(bf16[32,128,64]{1,2,0:T(8,128)(2,1)S(1)} %fusion.38), channel_id=1, source_target_pairs={{0,32},{8,40},{16,48},{24,56},{32,0},{40,8},{48,16},{56,24},{64,96... | collective-permute-start | bytes 1572872 | tf_op jit(solution)/shard_map/ppermute | solution.py:20
  553.1 6.0 collective-permute-start.6
  559.7 7.2 %collective-permute-start.8 = (bf16[32]{0:T(256)(128)(2,1)S(1)}, bf16[32]{0:T(256)(128)(2,1)S(1)}, u32[]{:S(2)}, u32[]{:S(2)}) collective-permute-start(bf16[32]{0:T(256)(128)(2,1)S(1)} %get-tuple-element.40), channel_id=1, source_target_pairs={{0,64},{8,72},{16,80},{24,88},{32,96},{40,104},{48,112},{56,120},{... | collective-permute-start | bytes 200 | tf_op jit(solution)/shard_map/ppermute | solution.py:20
  570.3 25.3 %collective-permute-start.7 = (bf16[32,128,64]{1,2,0:T(8,128)(2,1)}, bf16[32,128,64]{1,2,0:T(8,128)(2,1)S(1)}, u32[]{:S(2)}, u32[]{:S(2)}) collective-permute-start(bf16[32,128,64]{1,2,0:T(8,128)(2,1)} %fusion.37), channel_id=1, source_target_pairs={{0,64},{8,72},{16,80},{24,88},{32,96},{40,104},{48,112},{56,120},{... | collective-permute-start | bytes 1572872 | tf_op jit(solution)/shard_map/ppermute | solution.py:20
  598.2 28.4 %collective-permute-start.9 = (bf16[32,128,64]{1,2,0:T(8,128)(2,1)}, bf16[32,128,64]{1,2,0:T(8,128)(2,1)}, u32[]{:S(2)}, u32[]{:S(2)}) collective-permute-start(bf16[32,128,64]{1,2,0:T(8,128)(2,1)} %fusion.28), channel_id=1, source_target_pairs={{0,128},{8,136},{16,144},{24,152},{32,160},{40,168},{48,176},{56,1... | collective-permute-start | bytes 1572872 | tf_op jit(solution)/shard_map/ppermute | solution.py:20
  603.7 24.9 %copy-start.2 = (f32[32,128,64]{1,2,0:T(8,128)S(1)}, f32[32,128,64]{1,2,0:T(8,128)}, u32[]{:S(2)}) copy-start(f32[32,128,64]{1,2,0:T(8,128)} %get-tuple-element.26) | copy-start | bytes 3145732
  604.7 26.5 %slice-start.3 = ((f32[4,32,128,64]{2,3,1,0:T(8,128)}), f32[3,32,128,64]{2,3,1,0:T(8,128)S(1)}, s32[]{:S(2)}) async-start(f32[4,32,128,64]{2,3,1,0:T(8,128)} %copy-done.1), calls=%async_computation.4 | async-start | bytes 6291456 | tf_op jit(solution)/shard_map/slice | solution.py:85
  631.1 5.4 slice-start
  631.1 16.2 %slice-start.1 = ((s8[8388608]{0:T(1024)(128)(4,1)}), s8[4194304]{0:T(1024)(128)(4,1)S(1)}, s32[]{:S(2)}) async-start(s8[8388608]{0:T(1024)(128)(4,1)} %bitcast.70), calls=%async_computation.2 | async-start | bytes 8388608
  636.5 10.8 %slice-start.2 = ((s8[8388608]{0:T(1024)(128)(4,1)}), s8[4194304]{0:T(1024)(128)(4,1)S(1)}, s32[]{:S(2)}) async-start(s8[8388608]{0:T(1024)(128)(4,1)} %bitcast.70), calls=%async_computation.3 | async-start | bytes 8388608
  647.4 8.7 %copy-start.15 = (pred[8,64]{1,0:T(8,128)(4,1)S(1)}, pred[8,64]{1,0:T(8,128)(4,1)}, u32[]{:S(2)}) copy-start(pred[8,64]{1,0:T(8,128)(4,1)} %add_compare_fusion) | copy-start | bytes 1540
  (14 other events, 38.8 us)
